TPU v7x, 32 devices: a whole 2x2x4 slice. The times are simulated.
32 devices in a mesh: replica: 4 (over y, core), kvhead: 4 (over z), ffn: 2 (over x).
Axes of the slice: x: 2, y: 2, z: 4, core: 2. Of those that a mesh axis runs over, the one named last changes fastest.
Arguments:
- queries: bfloat16 [16, 16384], P('replica', 'kvhead'), may hold values from -400 to 400
- k_cache: bfloat16 [512, 64, 1024], P(('replica', 'ffn'), None, 'kvhead'), may hold values from -6 to 6
- v_cache: bfloat16 [512, 64, 1024], P(('replica', 'ffn'), None, 'kvhead'), may hold values from -6 to 6
- page_table: int32 [16, 32], P('replica', 'ffn'), may hold values from 0 to 63, as said below
- seq_lens: int32 [16], P('replica'), may hold values from 1 to 2048, as said below
- out_proj: bfloat16 [16384, 16384], P('kvhead', ('replica', 'ffn')), may hold values from -0.125 to 0.125
- residual: bfloat16 [16, 16384], P('kvhead', ('replica', 'ffn')), may hold values from -40 to 40
- norm_gain: bfloat16 [16384], P(('replica', 'ffn')), may hold values from 0.099609375 to 1.8984375
- gate_weight: bfloat16 [26624, 16384], P(('replica', 'kvhead', 'ffn')), may hold values from -0.046875 to 0.046875
- up_weight: bfloat16 [26624, 16384], P(('replica', 'kvhead', 'ffn')), may hold values from -0.046875 to 0.046875
Outputs:
- post_attn: bfloat16 [16, 16384], P('kvhead', ('replica', 'ffn'))
- hidden: bfloat16 [16, 26624], P(None, ('replica', 'kvhead', 'ffn'))
Inputs may be any that keep to these rules, and one draw needn't show every extreme that they name: `page_table`: over the 4 rows of one replica, the entries of page columns j with the same j // 16 name every pool page 0 to 63 exactly once. `seq_lens`: some row has length 2048.
All inputs are finite; a program needn't handle non-finite values.
Results may differ from a plain program's by a relative error of at most 0.0079.
Values may be sent and summed in bfloat16 or wider, within the bound.
A program may use at most 192 MiB of HBM per device.

v0:
```python
import math
import jax
import jax.numpy as jnp
from jax import lax
from jax.sharding import PartitionSpec as P

D = 16384
HD = 128
GQ = 16
NEG_FILL = -1e30
NORM_EPS = 1e-05


def merged(part, axis, combine):
    gathered = jax.tree.map(lambda a: lax.all_gather(a, axis), part)

    def take(source):
        return jax.tree.map(lambda a: lax.dynamic_index_in_dim(a, source, 0, False), gathered)

    return lax.fori_loop(
        1, lax.axis_size(axis), lambda source, state: combine(state, take(source)), take(0)
    )


def join_parts(earlier, later):
    first_max, first_total, first_out = earlier
    second_max, second_total, second_out = later
    overall = jnp.maximum(first_max, second_max)
    first_factor = jnp.exp(first_max - overall)
    second_factor = jnp.exp(second_max - overall)
    joined_total = first_total * first_factor + second_total * second_factor
    joined_out = first_out * first_factor[..., None] + second_out * second_factor[..., None]
    return (overall, joined_total, joined_out)


def per_device(
    queries,
    k_cache,
    v_cache,
    page_table,
    seq_lens,
    out_proj,
    residual,
    norm_gain,
    gate_weight,
    up_weight,
):
    score_scale = 1.0 / math.sqrt(HD)
    row_count = queries.shape[0]
    local_heads = k_cache.shape[2] // HD
    span_len = page_table.shape[1] * k_cache.shape[1]
    key_rows = k_cache[page_table].reshape(row_count, span_len, local_heads, HD)
    value_rows = v_cache[page_table].reshape(row_count, span_len, local_heads, HD)
    query_heads = queries.reshape(row_count, local_heads, GQ, HD)
    scores = (
        jnp.einsum("rkgd,rskd->rkgs", query_heads, key_rows, preferred_element_type=jnp.float32)
        * score_scale
    )
    positions = lax.axis_index("ffn") * span_len + jnp.arange(span_len, dtype=jnp.int32)
    visible = (positions[None, :] < seq_lens[:, None])[:, None, None, :]
    block_max = jnp.max(jnp.where(visible, scores, NEG_FILL), axis=-1)
    weights = jnp.where(visible, jnp.exp(scores - block_max[..., None]), 0.0)
    block_total = jnp.sum(weights, axis=-1)
    block_out = jnp.einsum(
        "rkgs,rskd->rkgd",
        weights.astype(jnp.bfloat16),
        value_rows,
        preferred_element_type=jnp.float32,
    )
    overall, denominator, weighted = merged((block_max, block_total, block_out), "ffn", join_parts)
    contexts = (
        (weighted / denominator[..., None])
        .astype(jnp.bfloat16)
        .reshape(row_count, local_heads * GQ * HD)
    )
    partial_value = jnp.dot(
        lax.all_gather(contexts, "replica", axis=0, tiled=True),
        out_proj,
        preferred_element_type=jnp.float32,
    )
    own_count = residual.shape[0]
    own_first = lax.axis_index("kvhead") * own_count
    own_part = lax.dynamic_slice_in_dim(partial_value, own_first, own_count, 0) + residual.astype(
        jnp.float32
    )
    partial_value = lax.dynamic_update_slice_in_dim(partial_value, own_part, own_first, 0)
    gain_wide = norm_gain.astype(jnp.float32)
    summed = lax.psum(partial_value, "kvhead")
    post_all = summed.astype(jnp.bfloat16)
    post_attn = lax.dynamic_slice_in_dim(post_all, own_first, own_count, 0)
    widened = post_all.astype(jnp.float32)
    squares = lax.psum(jnp.sum(widened * widened, axis=1), ("replica", "ffn"))
    normed = (widened * lax.rsqrt(squares / D + NORM_EPS)[:, None] * gain_wide).astype(jnp.bfloat16)
    contract = (((1,), (1,)), ((), ()))
    shard_cols = lax.all_gather(normed, ("replica", "ffn"), axis=1, tiled=True)
    gate_sum = lax.dot_general(
        shard_cols, gate_weight, contract, preferred_element_type=jnp.float32
    )
    up_sum = lax.dot_general(shard_cols, up_weight, contract, preferred_element_type=jnp.float32)
    hidden = (jax.nn.silu(gate_sum) * up_sum).astype(jnp.bfloat16)
    return (post_attn, hidden)


def solution(mesh):
    in_specs = (
        P("replica", "kvhead"),
        P(("replica", "ffn"), None, "kvhead"),
        P(("replica", "ffn"), None, "kvhead"),
        P("replica", "ffn"),
        P("replica"),
        P("kvhead", ("replica", "ffn")),
        P("kvhead", ("replica", "ffn")),
        P(("replica", "ffn")),
        P(("replica", "kvhead", "ffn"), None),
        P(("replica", "kvhead", "ffn"), None),
    )
    out_specs = (P("kvhead", ("replica", "ffn")), P(None, ("replica", "kvhead", "ffn")))
    return jax.shard_map(
        per_device, mesh=mesh, in_specs=in_specs, out_specs=out_specs, check_vma=False
    )
```

profile of v0, /device:TPU:1, one launch (start us, length us, event | category | flops | bytes accessed | tf_op | source)
XLA Modules:
  0.0 121.5 jit_solution(7688263210400951377)
XLA Ops:
  0.6 0.0 copy-start
  0.7 0.9 broadcast_compare_fusion
  1.5 0.7 compare_select_fusion
  2.2 0.1 reshape.100
  2.3 0.0 copy-done
  2.3 2.0 %gather_fusion = bf16[64,64,256]{2,1,0:T(8,128)(2,1)} fusion(bf16[64,64,256]{2,1,0:T(8,128)(2,1)S(1)} %copy-done, s32[1024]{0:T(1024)S(1)} %pad_clamp_fusion), kind=kCustom, calls=%fused_computation | custom fusion | bytes 4194560 | tf_op jit(solution)/shard_map/gather | solution.py:52
  4.4 0.0 copy-start.2
  4.4 2.6 %reshape.95 = bf16[4,1024,2,128]{3,2,1,0:T(2,128)(2,1)S(1)} reshape(bf16[64,64,256]{2,1,0:T(8,128)(2,1)} %gather_fusion) | data formatting | bytes 4194304 | tf_op jit(solution)/shard_map/reshape | solution.py:52
  6.9 0.0 copy-done.2
  6.9 0.7 select_reduce_fusion
  7.7 0.3 bitcast_reduce_fusion
  7.9 3.8 %all-gather.2 = f32[8,2,16]{2,1,0:T(2,128)S(1)} all-gather(f32[4,2,16]{2,1,0:T(2,128)S(1)} %bitcast_reduce_fusion), channel_id=4, replica_groups=mesh['replica'=4,'kvhead'=4,'ffn'=2] {'ffn'}, dimensions={0}, use_global_device_ids=true | all-gather | bytes 1536 | tf_op jit(solution)/shard_map/all_gather | solution.py:15
  11.7 3.2 %all-gather.1 = f32[8,2,16]{2,1,0:T(2,128)S(1)} all-gather(f32[4,2,16]{2,1,0:T(2,128)S(1)} %get-tuple-element.21), channel_id=3, replica_groups=mesh['replica'=4,'kvhead'=4,'ffn'=2] {'ffn'}, dimensions={0}, use_global_device_ids=true | all-gather | bytes 1536 | tf_op jit(solution)/shard_map/all_gather | solution.py:15
  14.9 2.3 %gather_fusion.1 = bf16[64,64,256]{2,1,0:T(8,128)(2,1)S(1)} fusion(bf16[64,64,256]{2,1,0:T(8,128)(2,1)} %param.12, s32[1024]{0:T(1024)S(1)} %pad_clamp_fusion), kind=kCustom, calls=%fused_computation.1 | custom fusion | bytes 4194560 | tf_op jit(solution)/shard_map/gather | solution.py:53
  17.2 2.1 %reshape.97 = bf16[4,1024,2,128]{3,2,1,0:T(2,128)(2,1)} reshape(bf16[64,64,256]{2,1,0:T(8,128)(2,1)S(1)} %gather_fusion.1) | data formatting | bytes 4194304 | tf_op jit(solution)/shard_map/reshape | solution.py:53
  19.3 2.0 %fusion = f32[4,2,16,128]{3,2,1,0:T(8,128)S(1)} fusion(bf16[4,1024,2,128]{3,2,1,0:T(2,128)(2,1)} %reshape.97, f32[4,2,1024,16]{2,3,1,0:T(8,128)S(1)} %get-tuple-element.22, f32[4,2,16]{2,1,0:T(2,128)S(1)} %get-tuple-element.21, pred[4,1024]{1,0:T(4,128)(4,1)S(1)} %broadcast_compare_fusion), kind=kOutput, calls=%fused_computation.2 | convolution fusion | flops 33947648 | bytes 2691584 | tf_op jit(solution)/shard_map/rkgs,rskd->rkgd/dot_general | solution.py:64
  21.3 3.8 %all-gather = f32[8,2,16,128]{3,2,1,0:T(8,128)S(1)} all-gather(f32[4,2,16,128]{3,2,1,0:T(8,128)S(1)} %fusion), channel_id=2, replica_groups=mesh['replica'=4,'kvhead'=4,'ffn'=2] {'ffn'}, dimensions={0}, use_global_device_ids=true | all-gather | bytes 196608 | tf_op jit(solution)/shard_map/all_gather | solution.py:15
  25.1 0.1 fusion.16
  25.3 9.3 %all-gather.3 = bf16[4,4,4096]{2,1,0:T(4,128)(2,1)S(1)} all-gather(bf16[1,4,4096]{2,1,0:T(4,128)(2,1)S(1)} %reshape.139), channel_id=1, replica_groups=mesh['replica'=4,'kvhead'=4,'ffn'=2] {'replica'}, dimensions={0}, use_global_device_ids=true | all-gather | bytes 163840 | tf_op jit(solution)/shard_map/all_gather | solution.py:77
  34.6 0.0 copy-start.3
  34.6 0.0 copy-start.4
  34.6 8.1 %fusion.23 = f32[16,2048]{1,0:T(8,128)S(1)} fusion(bf16[16,4096]{1,0:T(8,128)(2,1)S(1)} %reshape.140, bf16[4096,2048]{1,0:T(8,128)(2,1)} %param.15), kind=kOutput, calls=%fused_computation.41 | convolution fusion | flops 268435456 | bytes 17039360 | tf_op jit(solution)/shard_map/dot_general | solution.py:76
  42.7 0.0 copy-done.3
  42.7 17.8 %all-reduce.1 = bf16[16,2048]{1,0:T(8,128)(2,1)S(1)} all-reduce(f32[16,2048]{1,0:T(8,128)S(1)} %add_dynamic-update-slice_fusion), channel_id=1, replica_groups=mesh['replica'=4,'kvhead'=4,'ffn'=2] {'kvhead'}, use_global_device_ids=true, to_apply=%region_2.3 | all-reduce | flops 32768 | bytes 196608 | tf_op jit(solution)/shard_map/psum | solution.py:88
  60.5 0.1 fusion.11
  60.6 17.2 %psum.15 = f32[16]{0:T(128)S(1)} all-reduce(f32[16]{0:T(128)S(1)} %fusion.11), channel_id=1, replica_groups=mesh['replica'=4,'kvhead'=4,'ffn'=2] {'replica','ffn'}, use_global_device_ids=true, to_apply=%region_4.5 | all-reduce | flops 16 | bytes 128 | tf_op jit(solution)/shard_map/psum | solution.py:92
  77.8 0.0 copy-done.4
  77.8 0.1 fusion.13
  77.9 17.4 %all_gather.31 = bf16[16,16384]{1,0:T(8,128)(2,1)S(1)} all-gather(bf16[16,2048]{1,0:T(8,128)(2,1)S(1)} %fusion.13), channel_id=1, replica_groups=mesh['replica'=4,'kvhead'=4,'ffn'=2] {'replica','ffn'}, dimensions={1}, use_global_device_ids=true | all-gather | bytes 589824 | tf_op jit(solution)/shard_map/all_gather | solution.py:95
  95.3 12.4 %fusion.24 = f32[16,832]{1,0:T(8,128)S(1)} fusion(bf16[16,16384]{1,0:T(8,128)(2,1)S(1)} %all_gather.31, bf16[832,16384]{1,0:T(8,128)(2,1)} %param.18), kind=kOutput, calls=%fused_computation.42 | convolution fusion | flops 436207616 | bytes 27840512 | tf_op jit(solution)/shard_map/dot_general | solution.py:96
  107.7 0.0 copy-start.1
  107.7 13.2 %fusion.7 = bf16[16,832]{1,0:T(8,128)(2,1)} fusion(bf16[16,16384]{1,0:T(8,128)(2,1)S(1)} %all_gather.31, bf16[832,16384]{1,0:T(8,128)(2,1)} %param.19, f32[16,832]{1,0:T(8,128)S(1)} %fusion.24), kind=kOutput, calls=%fused_computation.8 | convolution fusion | flops 436287488 | bytes 27867136 | tf_op jit(solution)/shard_map/dot_general | solution.py:99
  120.9 0.6 constant_dynamic-slice_fusion
  121.5 0.0 copy-done.1
  (9 shorter events, 0.1 us)
Async XLA Ops:
  0.6 1.7 %copy-start = (bf16[64,64,256]{2,1,0:T(8,128)(2,1)S(1)}, bf16[64,64,256]{2,1,0:T(8,128)(2,1)}, u32[]{:S(2)}) copy-start(bf16[64,64,256]{2,1,0:T(8,128)(2,1)} %param.11) | copy-start | bytes 6291460
  4.4 2.6 %copy-start.2 = (bf16[4,4096]{1,0:T(4,128)(2,1)S(1)}, bf16[4,4096]{1,0:T(4,128)(2,1)}, u32[]{:S(2)}) copy-start(bf16[4,4096]{1,0:T(4,128)(2,1)} %param.10) | copy-start | bytes 98308
  34.6 8.1 %copy-start.3 = (bf16[4,2048]{1,0:T(4,128)(2,1)S(1)}, bf16[4,2048]{1,0:T(4,128)(2,1)}, u32[]{:S(2)}) copy-start(bf16[4,2048]{1,0:T(4,128)(2,1)} %param.16) | copy-start | bytes 49156
  34.6 43.2 %copy-start.4 = (bf16[2048]{0:T(1024)(128)(2,1)S(1)}, bf16[2048]{0:T(1024)(128)(2,1)}, u32[]{:S(2)}) copy-start(bf16[2048]{0:T(1024)(128)(2,1)} %param.17) | copy-start | bytes 12292
  107.7 13.8 %copy-start.1 = (bf16[64,64,256]{2,1,0:T(8,128)(2,1)S(1)}, bf16[64,64,256]{2,1,0:T(8,128)(2,1)}, u32[]{:S(2)}) copy-start(bf16[64,64,256]{2,1,0:T(8,128)(2,1)} %param.11) | copy-start | bytes 6291460
where the time goes:
time: 122 us; the launch traced here: 121 us
  blocking collectives  72.4 us (59%)
  matrix products  36.4 us (30%)
  local copies, waits for them, and re-layouts  9.74 us (8%)
  other arithmetic  2.21 us (2%)
    psum x1, blocking collectives, per_device(): summed = lax.psum(partial_value, 'kvhead')  17.8 us
    all_gather x1, blocking collectives, per_device(): shard_cols = lax.all_gather(normed, ('replica', 'ffn'), axis=1, tiled=True)  17.4 us
    psum x1, blocking collectives, per_device(): squares = lax.psum(jnp.sum(widened * widened, axis=1), ('replica', 'ffn'))  17.2 us
    dot_general x1, matrix products, per_device(): lax.dot_general(shard_cols, up_weight, contract, preferred_element_type=j...  13.2 us
    dot_general x1, matrix products, per_device(): lax.dot_general(shard_cols, gate_weight, contract, preferred_element_type...  12.4 us
    all_gather x3, blocking collectives, merged(): gathered = jax.tree.map(lambda a: lax.all_gather(a, axis), part)  10.7 us
    all_gather x1, blocking collectives, per_device(): lax.all_gather(contexts, 'replica', axis=0, tiled=True)  9.29 us
    dot_general x1, matrix products, per_device(): jnp.dot(lax.all_gather(contexts, 'replica', axis=0, tiled=True), out_proj...  8.05 us

commit v1 on v0

--- a/solution.py
+++ b/solution.py
@@ -85,7 +85,8 @@
     )
     partial_value = lax.dynamic_update_slice_in_dim(partial_value, own_part, own_first, 0)
     gain_wide = norm_gain.astype(jnp.float32)
-    summed = lax.psum(partial_value, "kvhead")
+    _attach_core = lambda base_x: jnp.sum(jax.lax.all_gather(base_x, "kvhead"), axis=0)
+    summed = _attach_core(partial_value)
     post_all = summed.astype(jnp.bfloat16)
     post_attn = lax.dynamic_slice_in_dim(post_all, own_first, own_count, 0)
     widened = post_all.astype(jnp.float32)

time: 122 us -> 117 us (0.959)
  blocking collectives: 72.4 us -> 67.2 us
    psum x1 -> x0, blocking collectives: 17.8 us -> none  [per_device(): summed = lax.psum(partial_value, 'kvhead')]
    all_gather x0 -> x1, blocking collectives: none -> 15.2 us  [per_device(): jax.lax.all_gather(base_x, 'kvhead')]
    psum x1, blocking collectives: 17.2 us -> 14.6 us  [per_device(): squares = lax.psum(jnp.sum(widened * widened, axis=1), ('replica', 'ffn'))]
where the time goes in v1:
time: 117 us; the launch traced here: 116 us
  blocking collectives  67.2 us (57%)
  matrix products  36.4 us (31%)
  local copies, waits for them, and re-layouts  9.75 us (8%)
  other arithmetic  2.24 us (2%)
    all_gather x1, blocking collectives, per_device(): shard_cols = lax.all_gather(normed, ('replica', 'ffn'), axis=1, tiled=True)  17.4 us
    all_gather x1, blocking collectives, per_device(): jax.lax.all_gather(base_x, 'kvhead')  15.2 us
    psum x1, blocking collectives, per_device(): squares = lax.psum(jnp.sum(widened * widened, axis=1), ('replica', 'ffn'))  14.6 us
    dot_general x1, matrix products, per_device(): lax.dot_general(shard_cols, up_weight, contract, preferred_element_type=j...  13.2 us
    dot_general x1, matrix products, per_device(): lax.dot_general(shard_cols, gate_weight, contract, preferred_element_type...  12.4 us
    all_gather x3, blocking collectives, merged(): gathered = jax.tree.map(lambda a: lax.all_gather(a, axis), part)  10.7 us
    all_gather x1, blocking collectives, per_device(): lax.all_gather(contexts, 'replica', axis=0, tiled=True)  9.29 us
    dot_general x1, matrix products, per_device(): jnp.dot(lax.all_gather(contexts, 'replica', axis=0, tiled=True), out_proj...  8.05 us

profile of v1, /device:TPU:1, one launch (start us, length us, event | category | flops | bytes accessed | tf_op | source)
XLA Modules:
  0.0 116.4 jit_solution(15870594650556119881)
XLA Ops:
  0.6 0.0 copy-start
  0.7 0.9 broadcast_compare_fusion
  1.5 0.7 compare_select_fusion
  2.2 0.1 reshape.102
  2.3 0.0 copy-done
  2.3 2.0 %gather_fusion = bf16[64,64,256]{2,1,0:T(8,128)(2,1)} fusion(bf16[64,64,256]{2,1,0:T(8,128)(2,1)S(1)} %copy-done, s32[1024]{0:T(1024)S(1)} %pad_clamp_fusion), kind=kCustom, calls=%fused_computation | custom fusion | bytes 4194560 | tf_op jit(solution)/shard_map/gather | solution.py:52
  4.4 0.0 copy-start.2
  4.4 2.6 %reshape.97 = bf16[4,1024,2,128]{3,2,1,0:T(2,128)(2,1)S(1)} reshape(bf16[64,64,256]{2,1,0:T(8,128)(2,1)} %gather_fusion) | data formatting | bytes 4194304 | tf_op jit(solution)/shard_map/reshape | solution.py:52
  6.9 0.0 copy-done.2
  6.9 0.7 select_reduce_fusion
  7.7 0.3 bitcast_reduce_fusion
  7.9 3.8 %all-gather.2 = f32[8,2,16]{2,1,0:T(2,128)S(1)} all-gather(f32[4,2,16]{2,1,0:T(2,128)S(1)} %bitcast_reduce_fusion), channel_id=4, replica_groups=mesh['replica'=4,'kvhead'=4,'ffn'=2] {'ffn'}, dimensions={0}, use_global_device_ids=true | all-gather | bytes 1536 | tf_op jit(solution)/shard_map/all_gather | solution.py:15
  11.7 3.2 %all-gather.1 = f32[8,2,16]{2,1,0:T(2,128)S(1)} all-gather(f32[4,2,16]{2,1,0:T(2,128)S(1)} %get-tuple-element.21), channel_id=3, replica_groups=mesh['replica'=4,'kvhead'=4,'ffn'=2] {'ffn'}, dimensions={0}, use_global_device_ids=true | all-gather | bytes 1536 | tf_op jit(solution)/shard_map/all_gather | solution.py:15
  14.9 2.3 %gather_fusion.1 = bf16[64,64,256]{2,1,0:T(8,128)(2,1)S(1)} fusion(bf16[64,64,256]{2,1,0:T(8,128)(2,1)} %param.12, s32[1024]{0:T(1024)S(1)} %pad_clamp_fusion), kind=kCustom, calls=%fused_computation.1 | custom fusion | bytes 4194560 | tf_op jit(solution)/shard_map/gather | solution.py:53
  17.2 2.1 %reshape.99 = bf16[4,1024,2,128]{3,2,1,0:T(2,128)(2,1)} reshape(bf16[64,64,256]{2,1,0:T(8,128)(2,1)S(1)} %gather_fusion.1) | data formatting | bytes 4194304 | tf_op jit(solution)/shard_map/reshape | solution.py:53
  19.3 2.0 %fusion = f32[4,2,16,128]{3,2,1,0:T(8,128)S(1)} fusion(bf16[4,1024,2,128]{3,2,1,0:T(2,128)(2,1)} %reshape.99, f32[4,2,1024,16]{2,3,1,0:T(8,128)S(1)} %get-tuple-element.22, f32[4,2,16]{2,1,0:T(2,128)S(1)} %get-tuple-element.21, pred[4,1024]{1,0:T(4,128)(4,1)S(1)} %broadcast_compare_fusion), kind=kOutput, calls=%fused_computation.2 | convolution fusion | flops 33947648 | bytes 2691584 | tf_op jit(solution)/shard_map/rkgs,rskd->rkgd/dot_general | solution.py:64
  21.3 3.8 %all-gather = f32[8,2,16,128]{3,2,1,0:T(8,128)S(1)} all-gather(f32[4,2,16,128]{3,2,1,0:T(8,128)S(1)} %fusion), channel_id=2, replica_groups=mesh['replica'=4,'kvhead'=4,'ffn'=2] {'ffn'}, dimensions={0}, use_global_device_ids=true | all-gather | bytes 196608 | tf_op jit(solution)/shard_map/all_gather | solution.py:15
  25.1 0.1 fusion.16
  25.3 9.3 %all-gather.3 = bf16[4,4,4096]{2,1,0:T(4,128)(2,1)S(1)} all-gather(bf16[1,4,4096]{2,1,0:T(4,128)(2,1)S(1)} %reshape.141), channel_id=1, replica_groups=mesh['replica'=4,'kvhead'=4,'ffn'=2] {'replica'}, dimensions={0}, use_global_device_ids=true | all-gather | bytes 163840 | tf_op jit(solution)/shard_map/all_gather | solution.py:77
  34.6 0.0 copy-start.3
  34.6 0.0 copy-start.4
  34.6 8.1 %fusion.23 = f32[16,2048]{1,0:T(8,128)S(1)} fusion(bf16[16,4096]{1,0:T(8,128)(2,1)S(1)} %reshape.142, bf16[4096,2048]{1,0:T(8,128)(2,1)} %param.15), kind=kOutput, calls=%fused_computation.41 | convolution fusion | flops 268435456 | bytes 17039360 | tf_op jit(solution)/shard_map/dot_general | solution.py:76
  42.7 0.0 copy-done.3
  42.7 15.2 %all_gather.41 = f32[4,16,2048]{2,1,0:T(8,128)S(1)} all-gather(f32[1,16,2048]{2,1,0:T(8,128)S(1)} %bitcast_dynamic-update-slice_fusion), channel_id=1, replica_groups=mesh['replica'=4,'kvhead'=4,'ffn'=2] {'kvhead'}, dimensions={0}, use_global_device_ids=true | all-gather | bytes 655360 | tf_op jit(solution)/shard_map/all_gather | solution.py:88
  58.0 0.1 fusion.11
  58.1 14.6 %psum.7 = f32[16]{0:T(128)S(1)} all-reduce(f32[16]{0:T(128)S(1)} %fusion.11), channel_id=1, replica_groups=mesh['replica'=4,'kvhead'=4,'ffn'=2] {'replica','ffn'}, use_global_device_ids=true, to_apply=%region_4.5 | all-reduce | flops 16 | bytes 128 | tf_op jit(solution)/shard_map/psum | solution.py:93
  72.7 0.0 copy-done.4
  72.7 0.1 fusion.13
  72.7 17.4 %all_gather.42 = bf16[16,16384]{1,0:T(8,128)(2,1)S(1)} all-gather(bf16[16,2048]{1,0:T(8,128)(2,1)S(1)} %fusion.13), channel_id=1, replica_groups=mesh['replica'=4,'kvhead'=4,'ffn'=2] {'replica','ffn'}, dimensions={1}, use_global_device_ids=true | all-gather | bytes 589824 | tf_op jit(solution)/shard_map/all_gather | solution.py:96
  90.2 12.4 %fusion.24 = f32[16,832]{1,0:T(8,128)S(1)} fusion(bf16[16,16384]{1,0:T(8,128)(2,1)S(1)} %all_gather.42, bf16[832,16384]{1,0:T(8,128)(2,1)} %param.18), kind=kOutput, calls=%fused_computation.42 | convolution fusion | flops 436207616 | bytes 27840512 | tf_op jit(solution)/shard_map/dot_general | solution.py:97
  102.6 0.0 copy-start.1
  102.6 13.2 %fusion.7 = bf16[16,832]{1,0:T(8,128)(2,1)} fusion(bf16[16,16384]{1,0:T(8,128)(2,1)S(1)} %all_gather.42, bf16[832,16384]{1,0:T(8,128)(2,1)} %param.19, f32[16,832]{1,0:T(8,128)S(1)} %fusion.24), kind=kOutput, calls=%fused_computation.8 | convolution fusion | flops 436287488 | bytes 27867136 | tf_op jit(solution)/shard_map/dot_general | solution.py:100
  115.7 0.6 constant_dynamic-slice_fusion
  116.4 0.0 copy-done.1
  (11 shorter events, 0.2 us)
Async XLA Ops:
  0.6 1.7 %copy-start = (bf16[64,64,256]{2,1,0:T(8,128)(2,1)S(1)}, bf16[64,64,256]{2,1,0:T(8,128)(2,1)}, u32[]{:S(2)}) copy-start(bf16[64,64,256]{2,1,0:T(8,128)(2,1)} %param.11) | copy-start | bytes 6291460
  4.4 2.6 %copy-start.2 = (bf16[4,4096]{1,0:T(4,128)(2,1)S(1)}, bf16[4,4096]{1,0:T(4,128)(2,1)}, u32[]{:S(2)}) copy-start(bf16[4,4096]{1,0:T(4,128)(2,1)} %param.10) | copy-start | bytes 98308
  34.6 8.1 %copy-start.3 = (bf16[4,2048]{1,0:T(4,128)(2,1)S(1)}, bf16[4,2048]{1,0:T(4,128)(2,1)}, u32[]{:S(2)}) copy-start(bf16[4,2048]{1,0:T(4,128)(2,1)} %param.16) | copy-start | bytes 49156
  34.6 38.1 %copy-start.4 = (bf16[2048]{0:T(1024)(128)(2,1)S(1)}, bf16[2048]{0:T(1024)(128)(2,1)}, u32[]{:S(2)}) copy-start(bf16[2048]{0:T(1024)(128)(2,1)} %param.17) | copy-start | bytes 12292
  102.6 13.8 %copy-start.1 = (bf16[64,64,256]{2,1,0:T(8,128)(2,1)S(1)}, bf16[64,64,256]{2,1,0:T(8,128)(2,1)}, u32[]{:S(2)}) copy-start(bf16[64,64,256]{2,1,0:T(8,128)(2,1)} %param.11) | copy-start | bytes 6291460
